TPU v7x, 32 devices: a whole 2x2x4 slice. The times are simulated.
32 devices in a mesh: groups: 2 (over x), cx: 16 (over z, y, core).
Axes of the slice: x: 2, y: 2, z: 4, core: 2. Of those that a mesh axis runs over, the one named last changes fastest.
Arguments:
- displacements: bfloat16 [512, 3, 5120], P(('groups', 'cx')), parts along dimension 0, may hold values from -6 to 6
- forces: bfloat16 [512, 3, 5120], P(('groups', 'cx')), parts along dimension 0, may hold values from -6 to 6
- phi: bfloat16 [160, 14, 192, 192], P(('groups', 'cx')), parts along dimension 0, may hold values from -0.125 to 0.125
- neighbours: int32 [80, 14], P('cx'), may hold values from 0 to 79, as said below
- cluster_atoms: int32 [80, 64], P('cx'), may hold values from 0 to 5119, as said below
- config_order: int32 [512], P('groups'), parts along dimension 0, may hold values from 0 to 255, each once
- weights: float32 [512], P('groups'), parts along dimension 0, may hold values from 0.02 to 0.3
Outputs:
- residual: bfloat16 [160, 192, 256], P(('groups', 'cx')), parts along dimension 0
- gradient: bfloat16 [160, 14, 192, 192], P(('groups', 'cx')), parts along dimension 0
There are 2 independent parts, one for each index of `groups`. A program takes and returns all parts, laid end to end along the dimension named above; an argument that names none is the same for every part. Nothing has to cross between parts.
Inputs may be any that keep to these rules, and one draw needn't show every extreme that they name: `neighbours`: cluster c lies in layer c // 5 of 16 periodic layers; its 14 blocks name distinct clusters of its own layer and the two layers beside it, wrapping at the ends. `cluster_atoms`: the clusters of layer j hold the atoms 5 * 64 * j to 5 * 64 * (j + 1) - 1, each once. `config_order`: each ensemble index once.
All inputs are finite; a program needn't handle non-finite values.
Results may differ from a plain program's by a relative error of at most 0.0085.
Values may be sent and summed in bfloat16 or wider, within the bound.
No kernel may reach another device: no remote copies, remote signals or barrier semaphores. Data moves between devices by JAX's collectives and lax.ppermute only.
A program may use at most 128 MiB of HBM per device.

v0:
```python
import jax
import jax.numpy as jnp
from jax import lax
from jax.sharding import PartitionSpec as P

ATOMS = 64
LAYER = 5


def with_halo(block, sides, width):
    for axis, dim in sides:
        count = lax.axis_size(axis)
        forward = [(i, i + 1) for i in range(count - 1)]
        forward.append((count - 1, 0))
        backward = [(target, source) for source, target in forward]
        low = lax.ppermute(
            lax.slice_in_dim(block, block.shape[dim] - width, None, axis=dim), axis, forward
        )
        high = lax.ppermute(lax.slice_in_dim(block, 0, width, axis=dim), axis, backward)
        block = jnp.concatenate([low, block, high], axis=dim)
    return block


def arrange(field, atom_map):
    picked = jnp.take(field, atom_map.reshape(-1), axis=2)
    picked = picked.reshape(field.shape[0], 3, atom_map.shape[0], atom_map.shape[1])
    return jnp.transpose(picked, (2, 1, 3, 0)).reshape(
        atom_map.shape[0], 3 * atom_map.shape[1], field.shape[0]
    )


def shards(displacements, forces, phi, neighbours, cluster_atoms, config_order, weights):
    axis_width = lax.axis_size("cx")
    position = lax.axis_index("cx")
    atom_local = cluster_atoms - position * (LAYER * ATOMS)
    layer_of = neighbours // LAYER
    offset = (layer_of - position + 1 + axis_width) % axis_width
    near_index = offset * LAYER + neighbours % LAYER
    moved_disp, moved_force = (
        lax.all_to_all(displacements, "cx", split_axis=2, concat_axis=0, tiled=True),
        lax.all_to_all(forces, "cx", split_axis=2, concat_axis=0, tiled=True),
    )
    cluster_force = arrange(moved_force, atom_local)
    cluster_disp = arrange(moved_disp, atom_local)
    framed_disp = with_halo(cluster_disp, (("cx", 0),), LAYER)
    beside_disp = jnp.take(framed_disp, near_index, axis=0)
    harmonic = jnp.einsum("ckij,ckjs->cis", phi, beside_disp, preferred_element_type=jnp.float32)
    residual = (cluster_force.astype(jnp.float32) + harmonic).astype(jnp.bfloat16)
    framed_resid = with_halo(residual, (("cx", 0),), LAYER)
    beside_resid = jnp.take(framed_resid, near_index, axis=0)
    match = config_order[:, None] == jnp.arange(config_order.shape[0], dtype=jnp.int32)[None, :]
    weight_row = jnp.sum(
        jnp.where(match, weights[None, :], jnp.zeros_like(weights)[None, :]), axis=1
    )
    wres = (residual.astype(jnp.float32) * weight_row[None, None, :]).astype(jnp.bfloat16)
    wdisp = (cluster_disp.astype(jnp.float32) * weight_row[None, None, :]).astype(jnp.bfloat16)
    first = jnp.einsum("cis,ckjs->ckij", wres, beside_disp, preferred_element_type=jnp.float32)
    second = jnp.einsum("cis,ckjs->ckij", wdisp, beside_resid, preferred_element_type=jnp.float32)
    summed = first + second
    gradient = (0.5 * summed).astype(jnp.bfloat16)
    return (residual, gradient)


def solution(mesh):
    in_specs = (
        P(("groups", "cx"), None, None),
        P(("groups", "cx"), None, None),
        P(("groups", "cx"), None, None, None),
        P("cx", None),
        P("cx", None),
        P("groups"),
        P("groups"),
    )
    out_specs = (P(("groups", "cx"), None, None), P(("groups", "cx"), None, None, None))
    return jax.shard_map(shards, mesh=mesh, in_specs=in_specs, out_specs=out_specs, check_vma=False)
```

profile of v0, /device:TPU:0, one launch (start us, length us, event | category | flops | bytes accessed | tf_op | source)
XLA Modules:
  0.0 138.1 jit_solution(12460175650179497296)
XLA Ops:
  0.6 0.0 copy-start.3
  0.6 0.0 copy-start.2
  0.6 6.5 %copy.46 = bf16[16,3,5120]{0,1,2:T(4,128)(2,1)} copy(bf16[16,3,5120]{2,0,1:T(8,128)(2,1)} %param.11) | data formatting | bytes 983040 | tf_op args[0]
  7.1 8.1 %reshape.93 = bf16[16,2,7680]{2,1,0:T(2,128)(2,1)} reshape(bf16[5120,3,16]{2,1,0:T(4,128)(2,1)} %bitcast.54) | data formatting | bytes 983040
  15.2 0.0 copy-start.4
  15.2 0.0 copy-start.5
  15.2 0.0 copy-start.6
  15.2 7.6 %all-to-all-start.1 = ((bf16[16,2,7680]{2,1,0:T(2,128)(2,1)}), bf16[16,2,7680]{2,1,0:T(2,128)(2,1)S(1)}, u32[]{:S(2)}, u32[]{:S(2)}) async-start(bf16[16,2,7680]{2,1,0:T(2,128)(2,1)} %reshape.93), calls=%async_computation.1 | async-start | bytes 983040 | tf_op jit(solution)/shard_map/all_to_all | solution.py:40
  22.8 0.0 copy-done.3
  22.8 0.1 reshape.33
  22.9 0.0 copy-done.2
  22.9 4.9 %copy.41 = bf16[16,3,5120]{0,1,2:T(4,128)(2,1)} copy(bf16[16,3,5120]{2,0,1:T(8,128)(2,1)S(1)} %copy-done.2) | data formatting | bytes 983040 | tf_op args[1]
  27.8 8.1 %reshape.91 = bf16[16,2,7680]{2,1,0:T(2,128)(2,1)} reshape(bf16[5120,3,16]{2,1,0:T(4,128)(2,1)} %bitcast.55) | data formatting | bytes 983040
  35.9 0.0 copy-done.4
  36.0 0.6 all-to-all-done.1
  36.5 5.5 %all-to-all-start = ((bf16[16,2,7680]{2,1,0:T(2,128)(2,1)}), bf16[16,2,7680]{2,1,0:T(2,128)(2,1)S(1)}, u32[]{:S(2)}, u32[]{:S(2)}) async-start(bf16[16,2,7680]{2,1,0:T(2,128)(2,1)} %reshape.91), calls=%async_computation | async-start | bytes 983040 | tf_op jit(solution)/shard_map/all_to_all | solution.py:41
  42.0 0.1 reshape.80
  42.1 0.0 copy-done.5
  42.1 0.0 copy-done.6
  42.1 0.2 select_reduce_fusion
  42.3 6.4 %reshape.94 = bf16[5120,3,16]{2,1,0:T(4,128)(2,1)} reshape(bf16[16,2,7680]{2,1,0:T(2,128)(2,1)S(1)} %all-to-all-done.1) | data formatting | bytes 983040
  48.7 5.9 %copy.47 = bf16[16,3,16,320]{3,0,2,1:T(8,128)(2,1)S(1)} copy(bf16[16,3,16,320]{0,1,3,2:T(4,128)(2,1)} %bitcast.52) | data formatting | bytes 983040 | tf_op jit(solution)/shard_map/all_to_all | solution.py:40
  54.6 0.7 copy.48
  55.3 2.3 %gather_fusion.1 = bf16[320,256,3]{1,2,0:T(4,128)(2,1)S(1)} fusion(bf16[256,3,320]{0,1,2:T(4,128)(2,1)S(1)} %copy.48, s32[1024]{0:T(1024)S(1)} %pad_clamp_fusion.1), kind=kCustom, calls=%fused_computation.2.clone | custom fusion | bytes 984320 | tf_op jit(solution)/shard_map/jit(_take)/gather | solution.py:25
  57.6 1.1 select_bitcast_fusion
  58.8 0.1 copy.49
  58.9 4.4 %collective-permute-start.1 = (bf16[5,192,256]{2,1,0:T(8,128)(2,1)S(1)}, bf16[5,192,256]{2,1,0:T(8,128)(2,1)}, u32[]{:S(2)}, u32[]{:S(2)}) collective-permute-start(bf16[5,192,256]{2,1,0:T(8,128)(2,1)S(1)} %bitcast.56), channel_id=1, source_target_pairs={{1,0},{2,1},{3,2},{4,3},{5,4},{6,5},{7,6},{8,7},{9,8},{10,9},{11,1... | collective-permute-start | bytes 1474568 | tf_op jit(solution)/shard_map/ppermute | solution.py:19
  63.3 0.0 collective-permute-start
  63.3 0.0 all-to-all-done
  63.3 6.4 %reshape.92 = bf16[5120,3,16]{2,1,0:T(4,128)(2,1)} reshape(bf16[16,2,7680]{2,1,0:T(2,128)(2,1)S(1)} %all-to-all-done) | data formatting | bytes 983040
  69.7 5.9 %copy.42 = bf16[16,3,16,320]{3,0,2,1:T(8,128)(2,1)S(1)} copy(bf16[16,3,16,320]{0,1,3,2:T(4,128)(2,1)} %bitcast.53) | data formatting | bytes 983040 | tf_op jit(solution)/shard_map/all_to_all | solution.py:41
  75.6 0.7 copy.43
  76.3 2.3 %gather_fusion = bf16[320,256,3]{1,2,0:T(4,128)(2,1)S(1)} fusion(bf16[256,3,320]{0,1,2:T(4,128)(2,1)S(1)} %copy.43, s32[1024]{0:T(1024)S(1)} %pad_clamp_fusion.1), kind=kCustom, calls=%fused_computation.clone | custom fusion | bytes 984320 | tf_op jit(solution)/shard_map/jit(_take)/gather | solution.py:25
  78.6 0.1 copy_select_fusion
  78.7 0.1 convert_bitcast_fusion
  78.8 0.1 copy.45
  78.9 0.0 collective-permute-done.1
  78.9 0.0 collective-permute-done
  78.9 1.3 pad_maximum_fusion
  80.3 6.7 %gather_fusion.2 = bf16[70,192,256]{2,1,0:T(8,128)(2,1)} fusion(bf16[15,192,256]{2,1,0:T(8,128)(2,1)S(1)} %pad_maximum_fusion, s32[1024]{0:T(1024)S(1)} %pad_clamp_fusion), kind=kCustom, calls=%fused_computation.1.clone | custom fusion | bytes 13762840 | tf_op jit(solution)/shard_map/jit(_take)/gather | solution.py:46
  87.0 0.0 copy-start
  87.0 7.2 %fusion.12 = bf16[5,192,256]{2,1,0:T(8,128)(2,1)S(1)} fusion(f32[5,192,256]{2,1,0:T(8,128)S(1)} %bitcast.64, bf16[5,14,192,192]{3,2,1,0:T(8,128)(2,1)} %param.13, bf16[5,14,192,256]{3,2,1,0:T(8,128)(2,1)} %bitcast.50, pred[5,14]{1,0:T(8,128)(4,1)S(1)} %get-tuple-element.14), kind=kOutput, calls=%fused_computation.18 | convolution fusion | flops 1325137920 | bytes 13516870 | tf_op jit(solution)/shard_map/ckij,ckjs->cis/dot_general | solution.py:47
  94.2 0.0 copy-start.1
  94.2 4.5 %collective-permute-start.3 = (bf16[5,192,256]{2,1,0:T(8,128)(2,1)S(1)}, bf16[5,192,256]{2,1,0:T(8,128)(2,1)S(1)}, u32[]{:S(2)}, u32[]{:S(2)}) collective-permute-start(bf16[5,192,256]{2,1,0:T(8,128)(2,1)S(1)} %fusion.12), channel_id=1, source_target_pairs={{1,0},{2,1},{3,2},{4,3},{5,4},{6,5},{7,6},{8,7},{9,8},{10,9},{11,1... | collective-permute-start | bytes 1474568 | tf_op jit(solution)/shard_map/ppermute | solution.py:19
  98.7 0.0 collective-permute-start.2
  98.7 0.0 copy-done
  98.7 7.0 %fusion.2 = f32[5,14,192,192]{3,2,1,0:T(8,128)} fusion(bf16[5,14,192,256]{3,2,1,0:T(8,128)(2,1)S(1)} %bitcast.51, pred[5,14]{1,0:T(8,128)(4,1)S(1)} %get-tuple-element.14, bf16[5,192,256]{2,1,0:T(8,128)(2,1)S(1)} %fusion.12, f32[256]{0:T(256)S(1)} %select_reduce_fusion), kind=kOutput, calls=%fused_computation.8 | convolution fusion | flops 1325383680 | bytes 17695814 | tf_op jit(solution)/shard_map/cis,ckjs->ckij/dot_general | solution.py:57
  105.7 0.0 collective-permute-done.3
  105.7 4.0 %collective-permute-done.2 = bf16[5,192,256]{2,1,0:T(8,128)(2,1)S(1)} collective-permute-done((bf16[5,192,256]{2,1,0:T(8,128)(2,1)S(1)}, bf16[5,192,256]{2,1,0:T(8,128)(2,1)S(1)}, u32[]{:S(2)}, u32[]{:S(2)}) %collective-permute-start.2) | collective-permute-done | bytes 491552 | tf_op jit(solution)/shard_map/ppermute | solution.py:16
  109.6 0.0 copy-done.1
  109.6 0.2 pad_maximum_fusion.1
  109.8 6.7 %gather_fusion.3 = bf16[70,192,256]{2,1,0:T(8,128)(2,1)} fusion(bf16[15,192,256]{2,1,0:T(8,128)(2,1)S(1)} %pad_maximum_fusion.1, s32[1024]{0:T(1024)S(1)} %pad_clamp_fusion), kind=kCustom, calls=%fused_computation.3.clone | custom fusion | bytes 13762840 | tf_op jit(solution)/shard_map/jit(_take)/gather | solution.py:50
  116.5 11.6 %fusion.4 = bf16[5,14,192,192]{2,3,1,0:T(8,128)(2,1)} fusion(f32[5,14,192,192]{3,2,1,0:T(8,128)} %fusion.2, bf16[5,14,192,256]{3,2,1,0:T(8,128)(2,1)} %bitcast.49, pred[5,14]{1,0:T(8,128)(4,1)S(1)} %get-tuple-element.14, bf16[5,192,256]{2,1,0:T(8,128)(2,1)S(1)} %bitcast.59, f32[256]{0:T(256)S(1)} %select_reduce_fusion), kind=kOutput, calls=%fused_computation.10 | convolution fusion | flops 1333125120 | bytes 22856774 | tf_op jit(solution)/shard_map/cis,ckjs->ckij/dot_general | solution.py:58
  128.1 10.0 %copy.51 = bf16[5,14,192,192]{3,2,1,0:T(8,128)(2,1)} copy(bf16[5,14,192,192]{2,3,1,0:T(8,128)(2,1)} %fusion.4) | data formatting | bytes 10321920
  (7 shorter events, 0.1 us)
Async XLA Ops:
  0.6 22.2 %copy-start.3 = (s32[5,64]{1,0:T(8,128)S(1)}, s32[5,64]{1,0:T(8,128)}, u32[]{:S(2)}) copy-start(s32[5,64]{1,0:T(8,128)} %param.15) | copy-start | bytes 3844
  0.6 22.3 %copy-start.2 = (bf16[16,3,5120]{2,0,1:T(8,128)(2,1)S(1)}, bf16[16,3,5120]{2,0,1:T(8,128)(2,1)}, u32[]{:S(2)}) copy-start(bf16[16,3,5120]{2,0,1:T(8,128)(2,1)} %param.12) | copy-start | bytes 1474564
  15.2 20.7 %copy-start.4 = (s32[5,14]{1,0:T(8,128)S(1)}, s32[5,14]{1,0:T(8,128)}, u32[]{:S(2)}) copy-start(s32[5,14]{1,0:T(8,128)} %param.14) | copy-start | bytes 844
  15.2 26.9 %copy-start.5 = (f32[256]{0:T(256)S(1)}, f32[256]{0:T(256)}, u32[]{:S(2)}) copy-start(f32[256]{0:T(256)} %param.17) | copy-start | bytes 3076
  15.2 26.9 %copy-start.6 = (s32[256]{0:T(256)S(1)}, s32[256]{0:T(256)}, u32[]{:S(2)}) copy-start(s32[256]{0:T(256)} %param.16) | copy-start | bytes 3076
  15.2 21.3 %all-to-all-start.1 = ((bf16[16,2,7680]{2,1,0:T(2,128)(2,1)}), bf16[16,2,7680]{2,1,0:T(2,128)(2,1)S(1)}, u32[]{:S(2)}, u32[]{:S(2)}) async-start(bf16[16,2,7680]{2,1,0:T(2,128)(2,1)} %reshape.93), calls=%async_computation.1 | async-start | bytes 983040 | tf_op jit(solution)/shard_map/all_to_all | solution.py:40
  36.5 26.8 %all-to-all-start = ((bf16[16,2,7680]{2,1,0:T(2,128)(2,1)}), bf16[16,2,7680]{2,1,0:T(2,128)(2,1)S(1)}, u32[]{:S(2)}, u32[]{:S(2)}) async-start(bf16[16,2,7680]{2,1,0:T(2,128)(2,1)} %reshape.91), calls=%async_computation | async-start | bytes 983040 | tf_op jit(solution)/shard_map/all_to_all | solution.py:41
  58.9 20.0 %collective-permute-start.1 = (bf16[5,192,256]{2,1,0:T(8,128)(2,1)S(1)}, bf16[5,192,256]{2,1,0:T(8,128)(2,1)}, u32[]{:S(2)}, u32[]{:S(2)}) collective-permute-start(bf16[5,192,256]{2,1,0:T(8,128)(2,1)S(1)} %bitcast.56), channel_id=1, source_target_pairs={{1,0},{2,1},{3,2},{4,3},{5,4},{6,5},{7,6},{8,7},{9,8},{10,9},{11,1... | collective-permute-start | bytes 1474568 | tf_op jit(solution)/shard_map/ppermute | solution.py:19
  63.3 15.6 %collective-permute-start = (bf16[5,192,256]{2,1,0:T(8,128)(2,1)S(1)}, bf16[5,192,256]{2,1,0:T(8,128)(2,1)}, u32[]{:S(2)}, u32[]{:S(2)}) collective-permute-start(bf16[5,192,256]{2,1,0:T(8,128)(2,1)S(1)} %bitcast.57), channel_id=1, source_target_pairs={{0,1},{1,2},{2,3},{3,4},{4,5},{5,6},{6,7},{7,8},{8,9},{9,10},{10,1... | collective-permute-start | bytes 1474568 | tf_op jit(solution)/shard_map/ppermute | solution.py:16
  87.0 11.7 %copy-start = (bf16[70,192,256]{2,1,0:T(8,128)(2,1)S(1)}, bf16[70,192,256]{2,1,0:T(8,128)(2,1)}, u32[]{:S(2)}) copy-start(bf16[70,192,256]{2,1,0:T(8,128)(2,1)} %gather_fusion.2) | copy-start | bytes 20643844
  94.2 15.5 %copy-start.1 = (bf16[5,192,256]{2,1,0:T(8,128)(2,1)}, bf16[5,192,256]{2,1,0:T(8,128)(2,1)S(1)}, u32[]{:S(2)}) copy-start(bf16[5,192,256]{2,1,0:T(8,128)(2,1)S(1)} %fusion.12) | copy-start | bytes 1474564
  94.2 11.5 %collective-permute-start.3 = (bf16[5,192,256]{2,1,0:T(8,128)(2,1)S(1)}, bf16[5,192,256]{2,1,0:T(8,128)(2,1)S(1)}, u32[]{:S(2)}, u32[]{:S(2)}) collective-permute-start(bf16[5,192,256]{2,1,0:T(8,128)(2,1)S(1)} %fusion.12), channel_id=1, source_target_pairs={{1,0},{2,1},{3,2},{4,3},{5,4},{6,5},{7,6},{8,7},{9,8},{10,9},{11,1... | collective-permute-start | bytes 1474568 | tf_op jit(solution)/shard_map/ppermute | solution.py:19
  98.7 11.0 %collective-permute-start.2 = (bf16[5,192,256]{2,1,0:T(8,128)(2,1)S(1)}, bf16[5,192,256]{2,1,0:T(8,128)(2,1)S(1)}, u32[]{:S(2)}, u32[]{:S(2)}) collective-permute-start(bf16[5,192,256]{2,1,0:T(8,128)(2,1)S(1)} %fusion.12), channel_id=1, source_target_pairs={{0,1},{1,2},{2,3},{3,4},{4,5},{5,6},{6,7},{7,8},{8,9},{9,10},{10,1... | collective-permute-start | bytes 1474568 | tf_op jit(solution)/shard_map/ppermute | solution.py:16
where the time goes:
time: 140 us; the launch traced here: 138 us
  local copies, waits for them, and re-layouts  82 us (59%)
  matrix products  25.8 us (18%)
  starting transfers between devices  21.9 us (16%)
  waiting for transfers between devices  4.55 us (3%)
  other arithmetic  3.08 us (2%)
    unnamed x21, local copies, waits for them, and re-layouts  50.4 us
    dot_general x1, matrix products, shards(): jnp.einsum('cis,ckjs->ckij', wdisp, beside_resid, preferred_element_type=...  11.6 us
    ppermute x2, starting transfers between devices, with_halo(): lax.ppermute(lax.slice_in_dim(block, 0, width, axis=dim), axis, backward)  8.88 us
    all_to_all x1, starting transfers between devices, shards(): lax.all_to_all(displacements, 'cx', split_axis=2, concat_axis=0, tiled=True)  7.55 us
    dot_general x1, matrix products, shards(): jnp.einsum('ckij,ckjs->cis', phi, beside_disp, preferred_element_type=jnp...  7.16 us
    dot_general x1, matrix products, shards(): jnp.einsum('cis,ckjs->ckij', wres, beside_disp, preferred_element_type=jn...  6.97 us
    gather x1, local copies, waits for them, and re-layouts, shards(): beside_resid = jnp.take(framed_resid, near_index, axis=0)  6.72 us
    gather x1, local copies, waits for them, and re-layouts, shards(): beside_disp = jnp.take(framed_disp, near_index, axis=0)  6.72 us
  transfers between devices with their start and end apart: 6, of which 2 were waited for; matrix products, arithmetic and copies ran while one was open for 38% of the time, Pallas kernels for 0%

commit v1 on v0

--- a/solution.py
+++ b/solution.py
@@ -38,7 +38,10 @@
     near_index = offset * LAYER + neighbours % LAYER
     moved_disp, moved_force = (
         lax.all_to_all(displacements, "cx", split_axis=2, concat_axis=0, tiled=True),
-        lax.all_to_all(forces, "cx", split_axis=2, concat_axis=0, tiled=True),
+        jnp.concatenate(
+            lax.all_to_all(jnp.stack(jnp.split(forces, lax.axis_size("cx"), axis=2)), "cx", 0, 0),
+            axis=0,
+        ),
     )
     cluster_force = arrange(moved_force, atom_local)
     cluster_disp = arrange(moved_disp, atom_local)

time: 140 us -> 129 us (0.921)
  local copies, waits for them, and re-layouts: 82 us -> 67.2 us
  waiting for transfers between devices: 4.55 us -> 14.6 us
  starting transfers between devices: 21.9 us -> 16.4 us
    unnamed x21 -> x33, local copies, waits for them, and re-layouts: 50.4 us -> 40.8 us
    all_to_all x2 -> x1, local copies, waits for them, and re-layouts: 6.59 us -> 0.06 us  [shards(): lax.all_to_all(jnp.stack(jnp.split(forces, lax.axis_size('cx'), axis=2)),...]
    ppermute x2, waiting for transfers between devices: 3.98 us -> 8.52 us  [with_halo(): lax.ppermute(lax.slice_in_dim(block, block.shape[dim] - width, None, axis...]
    ppermute x2, starting transfers between devices: 8.88 us -> 4.54 us  [with_halo(): lax.ppermute(lax.slice_in_dim(block, 0, width, axis=dim), axis, backward)]
    ppermute x2, waiting for transfers between devices: 0.01 us -> 2.93 us  [with_halo(): lax.ppermute(lax.slice_in_dim(block, 0, width, axis=dim), axis, backward)]
    all_to_all x1, waiting for transfers between devices: 0.57 us -> 3.12 us  [shards(): lax.all_to_all(displacements, 'cx', split_axis=2, concat_axis=0, tiled=True)]
    all_to_all x1, starting transfers between devices: 5.45 us -> 3.99 us  [shards(): lax.all_to_all(jnp.stack(jnp.split(forces, lax.axis_size('cx'), axis=2)),...]
  transfers between devices with their start and end apart: 6 -> 6, of which waited for: 2 -> 4; matrix products, arithmetic and copies ran while one was open for 38% -> 30% of each run, Pallas kernels for 0% -> 0%
where the time goes in v1:
time: 129 us; the launch traced here: 128 us
  local copies, waits for them, and re-layouts  67.2 us (52%)
  matrix products  25.8 us (20%)
  starting transfers between devices  16.4 us (13%)
  waiting for transfers between devices  14.6 us (11%)
  other arithmetic  3.08 us (2%)
    unnamed x33, local copies, waits for them, and re-layouts  40.8 us
    dot_general x1, matrix products, shards(): jnp.einsum('cis,ckjs->ckij', wdisp, beside_resid, preferred_element_type=...  11.6 us
    ppermute x2, waiting for transfers between devices, with_halo(): lax.ppermute(lax.slice_in_dim(block, block.shape[dim] - width, None, axis...  8.52 us
    all_to_all x1, starting transfers between devices, shards(): lax.all_to_all(displacements, 'cx', split_axis=2, concat_axis=0, tiled=True)  7.41 us
    dot_general x1, matrix products, shards(): jnp.einsum('ckij,ckjs->cis', phi, beside_disp, preferred_element_type=jnp...  7.16 us
    dot_general x1, matrix products, shards(): jnp.einsum('cis,ckjs->ckij', wres, beside_disp, preferred_element_type=jn...  6.97 us
    gather x1, local copies, waits for them, and re-layouts, shards(): beside_resid = jnp.take(framed_resid, near_index, axis=0)  6.72 us
    gather x1, local copies, waits for them, and re-layouts, shards(): beside_disp = jnp.take(framed_disp, near_index, axis=0)  6.72 us
  transfers between devices with their start and end apart: 6, of which 4 were waited for; matrix products, arithmetic and copies ran while one was open for 30% of the time, Pallas kernels for 0%

profile of v1, /device:TPU:0, one launch (start us, length us, event | category | flops | bytes accessed | tf_op | source)
XLA Modules:
  0.0 127.9 jit_solution(17757981557728947074)
XLA Ops:
  0.6 0.0 copy-start.3
  0.6 0.0 copy-start.2
  0.7 0.0 copy-start.4
  0.7 0.0 copy-start.5
  0.7 0.0 copy-start.6
  0.7 6.5 %copy.43 = bf16[16,3,5120]{0,1,2:T(4,128)(2,1)} copy(bf16[16,3,5120]{2,0,1:T(8,128)(2,1)} %param.11) | data formatting | bytes 983040 | tf_op args[0]
  7.2 8.1 %reshape.95 = bf16[16,2,7680]{2,1,0:T(2,128)(2,1)} reshape(bf16[5120,3,16]{2,1,0:T(4,128)(2,1)} %bitcast.80) | data formatting | bytes 983040
  15.3 7.4 %all-to-all-start.1 = ((bf16[16,2,7680]{2,1,0:T(2,128)(2,1)}), bf16[16,2,7680]{2,1,0:T(2,128)(2,1)S(1)}, u32[]{:S(2)}, u32[]{:S(2)}) async-start(bf16[16,2,7680]{2,1,0:T(2,128)(2,1)} %reshape.95), calls=%async_computation.1 | async-start | bytes 983040 | tf_op jit(solution)/shard_map/all_to_all | solution.py:40
  22.7 0.0 copy-done.3
  22.7 0.0 copy-done.2
  22.7 0.6 bitcast_dynamic-update-slice_fusion.15
  23.4 0.7 bitcast_dynamic-update-slice_fusion.14
  24.1 0.6 bitcast_dynamic-update-slice_fusion.13
  24.7 0.7 bitcast_dynamic-update-slice_fusion.12
  25.4 0.6 bitcast_dynamic-update-slice_fusion.11
  26.0 0.7 bitcast_dynamic-update-slice_fusion.10
  26.7 0.6 bitcast_dynamic-update-slice_fusion.9
  27.3 0.7 bitcast_dynamic-update-slice_fusion.8
  28.0 0.6 bitcast_dynamic-update-slice_fusion.7
  28.6 0.7 bitcast_dynamic-update-slice_fusion.6
  29.3 0.6 bitcast_dynamic-update-slice_fusion.5
  29.9 0.7 bitcast_dynamic-update-slice_fusion.4
  30.6 0.0 copy-done.4
  30.6 0.1 reshape.37
  30.7 0.6 bitcast_dynamic-update-slice_fusion.3
  31.3 0.7 bitcast_dynamic-update-slice_fusion.2
  32.0 0.6 bitcast_dynamic-update-slice_fusion.1
  32.6 0.7 bitcast_dynamic-update-slice_fusion
  33.3 3.1 %all-to-all-done.1 = bf16[16,2,7680]{2,1,0:T(2,128)(2,1)S(1)} async-done(((bf16[16,2,7680]{2,1,0:T(2,128)(2,1)}), bf16[16,2,7680]{2,1,0:T(2,128)(2,1)S(1)}, u32[]{:S(2)}, u32[]{:S(2)}) %all-to-all-start.1) | async-done | bytes 491552 | tf_op jit(solution)/shard_map/all_to_all | solution.py:40
  36.4 4.0 %all-to-all-start = ((bf16[16,16,3,320]{3,1,2,0:T(8,128)(2,1)}), bf16[16,16,3,320]{3,1,2,0:T(8,128)(2,1)S(1)}, u32[]{:S(2)}, u32[]{:S(2)}) async-start(bf16[16,16,3,320]{3,1,2,0:T(8,128)(2,1)} %bitcast_dynamic-update-slice_fusion), calls=%async_computation | async-start | bytes 1179648 | tf_op jit(solution)/shard_map/all_to_all | solution.py:42
  40.4 0.1 reshape.84
  40.5 0.0 copy-done.5
  40.5 0.0 copy-done.6
  40.5 0.2 select_reduce_fusion
  40.7 6.4 %reshape.96 = bf16[5120,3,16]{2,1,0:T(4,128)(2,1)} reshape(bf16[16,2,7680]{2,1,0:T(2,128)(2,1)S(1)} %all-to-all-done.1) | data formatting | bytes 983040
  47.1 5.9 %copy.44 = bf16[16,3,16,320]{3,0,2,1:T(8,128)(2,1)S(1)} copy(bf16[16,3,16,320]{0,1,3,2:T(4,128)(2,1)} %bitcast.79) | data formatting | bytes 983040 | tf_op jit(solution)/shard_map/all_to_all | solution.py:40
  53.0 0.7 copy.45
  53.7 2.3 %gather_fusion.1 = bf16[320,256,3]{1,2,0:T(4,128)(2,1)S(1)} fusion(bf16[256,3,320]{0,1,2:T(4,128)(2,1)S(1)} %copy.45, s32[1024]{0:T(1024)S(1)} %pad_clamp_fusion.1), kind=kCustom, calls=%fused_computation.2.clone | custom fusion | bytes 984320 | tf_op jit(solution)/shard_map/jit(_take)/gather | solution.py:25
  56.1 1.1 select_bitcast_fusion
  57.2 0.1 copy.46
  57.3 4.4 %collective-permute-start.1 = (bf16[5,192,256]{2,1,0:T(8,128)(2,1)S(1)}, bf16[5,192,256]{2,1,0:T(8,128)(2,1)}, u32[]{:S(2)}, u32[]{:S(2)}) collective-permute-start(bf16[5,192,256]{2,1,0:T(8,128)(2,1)S(1)} %bitcast.81), channel_id=1, source_target_pairs={{1,0},{2,1},{3,2},{4,3},{5,4},{6,5},{7,6},{8,7},{9,8},{10,9},{11,1... | collective-permute-start | bytes 1474568 | tf_op jit(solution)/shard_map/ppermute | solution.py:19
  61.7 0.0 collective-permute-start
  61.7 0.0 all-to-all-done
  61.7 0.1 copy.39
  61.8 0.7 copy.40
  62.5 2.3 %gather_fusion = bf16[320,256,3]{1,2,0:T(4,128)(2,1)S(1)} fusion(bf16[256,3,320]{0,1,2:T(4,128)(2,1)S(1)} %copy.40, s32[1024]{0:T(1024)S(1)} %pad_clamp_fusion.1), kind=kCustom, calls=%fused_computation.clone | custom fusion | bytes 984320 | tf_op jit(solution)/shard_map/jit(_take)/gather | solution.py:25
  64.8 0.1 copy_select_fusion
  64.9 0.1 convert_bitcast_fusion
  65.0 0.1 copy.42
  65.1 2.9 %collective-permute-done.1 = bf16[5,192,256]{2,1,0:T(8,128)(2,1)} collective-permute-done((bf16[5,192,256]{2,1,0:T(8,128)(2,1)S(1)}, bf16[5,192,256]{2,1,0:T(8,128)(2,1)}, u32[]{:S(2)}, u32[]{:S(2)}) %collective-permute-start.1) | collective-permute-done | bytes 491552 | tf_op jit(solution)/shard_map/ppermute | solution.py:19
  68.1 4.7 %collective-permute-done = bf16[5,192,256]{2,1,0:T(8,128)(2,1)} collective-permute-done((bf16[5,192,256]{2,1,0:T(8,128)(2,1)S(1)}, bf16[5,192,256]{2,1,0:T(8,128)(2,1)}, u32[]{:S(2)}, u32[]{:S(2)}) %collective-permute-start) | collective-permute-done | bytes 491552 | tf_op jit(solution)/shard_map/ppermute | solution.py:16
  72.8 1.3 %pad_maximum_fusion = bf16[15,192,256]{2,1,0:T(8,128)(2,1)S(1)} fusion(bf16[5,192,256]{2,1,0:T(8,128)(2,1)} %collective-permute-done.1, bf16[5,192,256]{2,1,0:T(8,128)(2,1)S(1)} %bitcast.83, bf16[5,192,256]{2,1,0:T(8,128)(2,1)} %collective-permute-done), kind=kLoop, calls=%fused_computation.14 | loop fusion | flops 1474560 | bytes 2949120 | tf_op jit(solution)/shard_map/concatenate | solution.py:20
  74.1 6.7 %gather_fusion.2 = bf16[70,192,256]{2,1,0:T(8,128)(2,1)} fusion(bf16[15,192,256]{2,1,0:T(8,128)(2,1)S(1)} %pad_maximum_fusion, s32[1024]{0:T(1024)S(1)} %pad_clamp_fusion), kind=kCustom, calls=%fused_computation.1.clone | custom fusion | bytes 13762840 | tf_op jit(solution)/shard_map/jit(_take)/gather | solution.py:49
  80.8 7.2 %fusion.12 = bf16[5,192,256]{2,1,0:T(8,128)(2,1)S(1)} fusion(f32[5,192,256]{2,1,0:T(8,128)S(1)} %bitcast.89, bf16[5,14,192,192]{3,2,1,0:T(8,128)(2,1)} %param.13, bf16[5,14,192,256]{3,2,1,0:T(8,128)(2,1)} %bitcast.77, pred[5,14]{1,0:T(8,128)(4,1)S(1)} %get-tuple-element.14), kind=kOutput, calls=%fused_computation.18 | convolution fusion | flops 1325137920 | bytes 13516870 | tf_op jit(solution)/shard_map/ckij,ckjs->cis/dot_general | solution.py:50
  88.0 0.0 copy-start.1
  88.0 0.1 collective-permute-start.3
  88.2 0.4 collective-permute-start.2
  88.6 7.0 %fusion.2 = f32[5,14,192,192]{3,2,1,0:T(8,128)} fusion(bf16[5,14,192,256]{3,2,1,0:T(8,128)(2,1)S(1)} %bitcast.78, pred[5,14]{1,0:T(8,128)(4,1)S(1)} %get-tuple-element.14, bf16[5,192,256]{2,1,0:T(8,128)(2,1)S(1)} %fusion.12, f32[256]{0:T(256)S(1)} %select_reduce_fusion), kind=kOutput, calls=%fused_computation.8 | convolution fusion | flops 1325383680 | bytes 17695814 | tf_op jit(solution)/shard_map/cis,ckjs->ckij/dot_general | solution.py:60
  95.6 0.0 collective-permute-done.3
  95.6 3.8 %collective-permute-done.2 = bf16[5,192,256]{2,1,0:T(8,128)(2,1)S(1)} collective-permute-done((bf16[5,192,256]{2,1,0:T(8,128)(2,1)S(1)}, bf16[5,192,256]{2,1,0:T(8,128)(2,1)S(1)}, u32[]{:S(2)}, u32[]{:S(2)}) %collective-permute-start.2) | collective-permute-done | bytes 491552 | tf_op jit(solution)/shard_map/ppermute | solution.py:16
  99.4 0.2 pad_maximum_fusion.1
  99.5 6.7 %gather_fusion.3 = bf16[70,192,256]{2,1,0:T(8,128)(2,1)} fusion(bf16[15,192,256]{2,1,0:T(8,128)(2,1)S(1)} %pad_maximum_fusion.1, s32[1024]{0:T(1024)S(1)} %pad_clamp_fusion), kind=kCustom, calls=%fused_computation.3.clone | custom fusion | bytes 13762840 | tf_op jit(solution)/shard_map/jit(_take)/gather | solution.py:53
  106.3 11.6 %fusion.4 = bf16[5,14,192,192]{2,3,1,0:T(8,128)(2,1)} fusion(f32[5,14,192,192]{3,2,1,0:T(8,128)} %fusion.2, bf16[5,14,192,256]{3,2,1,0:T(8,128)(2,1)} %bitcast.76, pred[5,14]{1,0:T(8,128)(4,1)S(1)} %get-tuple-element.14, bf16[5,192,256]{2,1,0:T(8,128)(2,1)S(1)} %bitcast.84, f32[256]{0:T(256)S(1)} %select_reduce_fusion), kind=kOutput, calls=%fused_computation.10 | convolution fusion | flops 1333125120 | bytes 22856774 | tf_op jit(solution)/shard_map/cis,ckjs->ckij/dot_general | solution.py:61
  117.9 10.0 %copy.48 = bf16[5,14,192,192]{3,2,1,0:T(8,128)(2,1)} copy(bf16[5,14,192,192]{2,3,1,0:T(8,128)(2,1)} %fusion.4) | data formatting | bytes 10321920
  (10 shorter events, 0.1 us)
Async XLA Ops:
  0.6 22.1 %copy-start.3 = (s32[5,14]{1,0:T(8,128)S(1)}, s32[5,14]{1,0:T(8,128)}, u32[]{:S(2)}) copy-start(s32[5,14]{1,0:T(8,128)} %param.14) | copy-start | bytes 844
  0.6 22.1 %copy-start.2 = (bf16[16,3,5120]{2,0,1:T(8,128)(2,1)S(1)}, bf16[16,3,5120]{2,0,1:T(8,128)(2,1)}, u32[]{:S(2)}) copy-start(bf16[16,3,5120]{2,0,1:T(8,128)(2,1)} %param.12) | copy-start | bytes 1474564
  0.7 30.0 %copy-start.4 = (s32[5,64]{1,0:T(8,128)S(1)}, s32[5,64]{1,0:T(8,128)}, u32[]{:S(2)}) copy-start(s32[5,64]{1,0:T(8,128)} %param.15) | copy-start | bytes 3844
  0.7 39.9 %copy-start.5 = (f32[256]{0:T(256)S(1)}, f32[256]{0:T(256)}, u32[]{:S(2)}) copy-start(f32[256]{0:T(256)} %param.17) | copy-start | bytes 3076
  0.7 39.9 %copy-start.6 = (s32[256]{0:T(256)S(1)}, s32[256]{0:T(256)}, u32[]{:S(2)}) copy-start(s32[256]{0:T(256)} %param.16) | copy-start | bytes 3076
  15.3 21.2 %all-to-all-start.1 = ((bf16[16,2,7680]{2,1,0:T(2,128)(2,1)}), bf16[16,2,7680]{2,1,0:T(2,128)(2,1)S(1)}, u32[]{:S(2)}, u32[]{:S(2)}) async-start(bf16[16,2,7680]{2,1,0:T(2,128)(2,1)} %reshape.95), calls=%async_computation.1 | async-start | bytes 983040 | tf_op jit(solution)/shard_map/all_to_all | solution.py:40
  36.4 25.3 %all-to-all-start = ((bf16[16,16,3,320]{3,1,2,0:T(8,128)(2,1)}), bf16[16,16,3,320]{3,1,2,0:T(8,128)(2,1)S(1)}, u32[]{:S(2)}, u32[]{:S(2)}) async-start(bf16[16,16,3,320]{3,1,2,0:T(8,128)(2,1)} %bitcast_dynamic-update-slice_fusion), calls=%async_computation | async-start | bytes 1179648 | tf_op jit(solution)/shard_map/all_to_all | solution.py:42
  57.3 10.7 %collective-permute-start.1 = (bf16[5,192,256]{2,1,0:T(8,128)(2,1)S(1)}, bf16[5,192,256]{2,1,0:T(8,128)(2,1)}, u32[]{:S(2)}, u32[]{:S(2)}) collective-permute-start(bf16[5,192,256]{2,1,0:T(8,128)(2,1)S(1)} %bitcast.81), channel_id=1, source_target_pairs={{1,0},{2,1},{3,2},{4,3},{5,4},{6,5},{7,6},{8,7},{9,8},{10,9},{11,1... | collective-permute-start | bytes 1474568 | tf_op jit(solution)/shard_map/ppermute | solution.py:19
  61.7 11.1 %collective-permute-start = (bf16[5,192,256]{2,1,0:T(8,128)(2,1)S(1)}, bf16[5,192,256]{2,1,0:T(8,128)(2,1)}, u32[]{:S(2)}, u32[]{:S(2)}) collective-permute-start(bf16[5,192,256]{2,1,0:T(8,128)(2,1)S(1)} %bitcast.82), channel_id=1, source_target_pairs={{0,1},{1,2},{2,3},{3,4},{4,5},{5,6},{6,7},{7,8},{8,9},{9,10},{10,1... | collective-permute-start | bytes 1474568 | tf_op jit(solution)/shard_map/ppermute | solution.py:16
  80.8 7.7 %copy-start = (bf16[70,192,256]{2,1,0:T(8,128)(2,1)S(1)}, bf16[70,192,256]{2,1,0:T(8,128)(2,1)}, u32[]{:S(2)}) copy-start(bf16[70,192,256]{2,1,0:T(8,128)(2,1)} %gather_fusion.2) | copy-start | bytes 20643844
  88.0 11.4 %copy-start.1 = (bf16[5,192,256]{2,1,0:T(8,128)(2,1)}, bf16[5,192,256]{2,1,0:T(8,128)(2,1)S(1)}, u32[]{:S(2)}) copy-start(bf16[5,192,256]{2,1,0:T(8,128)(2,1)S(1)} %fusion.12) | copy-start | bytes 1474564
  88.0 7.5 %collective-permute-start.3 = (bf16[5,192,256]{2,1,0:T(8,128)(2,1)S(1)}, bf16[5,192,256]{2,1,0:T(8,128)(2,1)S(1)}, u32[]{:S(2)}, u32[]{:S(2)}) collective-permute-start(bf16[5,192,256]{2,1,0:T(8,128)(2,1)S(1)} %fusion.12), channel_id=1, source_target_pairs={{1,0},{2,1},{3,2},{4,3},{5,4},{6,5},{7,6},{8,7},{9,8},{10,9},{11,1... | collective-permute-start | bytes 1474568 | tf_op jit(solution)/shard_map/ppermute | solution.py:19
  88.2 11.2 %collective-permute-start.2 = (bf16[5,192,256]{2,1,0:T(8,128)(2,1)S(1)}, bf16[5,192,256]{2,1,0:T(8,128)(2,1)S(1)}, u32[]{:S(2)}, u32[]{:S(2)}) collective-permute-start(bf16[5,192,256]{2,1,0:T(8,128)(2,1)S(1)} %fusion.12), channel_id=1, source_target_pairs={{0,1},{1,2},{2,3},{3,4},{4,5},{5,6},{6,7},{7,8},{8,9},{9,10},{10,1... | collective-permute-start | bytes 1474568 | tf_op jit(solution)/shard_map/ppermute | solution.py:16
